TPU v7x, 256 devices: a whole 4x4x8 slice. The times are simulated.
256 devices in a mesh: sp: 64 (over y, z, core), dp: 4 (over x).
Axes of the slice: x: 4, y: 4, z: 8, core: 2. Of those that a mesh axis runs over, the one named last changes fastest.
Arguments:
- volume: bfloat16 [4, 96, 256, 8, 128], P('dp', None, 'sp'), may hold values from -6 to 6
- cotangent: bfloat16 [4, 96, 256, 8, 128], P('dp', None, 'sp'), may hold values from -6 to 6
- kernels_xy: bfloat16 [2, 96, 3, 3], replicated, may hold values from -2 to 2
- kernels_z: bfloat16 [2, 96, 3], replicated, may hold values from -3.5 to 3.5
- mixing: bfloat16 [2, 96, 96], replicated, may hold values from -0.625 to 0.625
Outputs:
- volume_grad: bfloat16 [4, 96, 256, 8, 128], P('dp', None, 'sp')
- mixing_grad: float32 [2, 96, 96], replicated
- xy_grad: float32 [2, 96, 3, 3], replicated
- z_grad: float32 [2, 96, 3], replicated
All inputs are finite; a program needn't handle non-finite values.
Results may differ from a plain program's by a relative error of at most 0.018.
Values may be sent and summed in bfloat16 or wider, within the bound.
A program may use at most 64 MiB of HBM per device.

v0:
```python
import math
import jax
import jax.numpy as jnp
from jax import lax
from jax.sharding import PartitionSpec as P


def padded_2(x, sides, width):
    for axis, dim in sides:
        count, length = (lax.axis_size(axis), x.shape[dim])
        up = [(i, (i + 1) % count) for i in range(count - 1)]
        down = [(j, i) for i, j in up]
        last = lax.slice_in_dim(x, length - width, length, axis=dim)
        first = lax.slice_in_dim(x, 0, width, axis=dim)
        before = lax.ppermute(last, axis, up)
        after = lax.ppermute(first, axis, down)
        x = jnp.concatenate([before, x, after], axis=dim)
    return x


def conv_plane(inputs, kernel):
    extent = inputs.shape[1] - 2
    across = inputs.shape[3]
    padded = jnp.pad(inputs, ((0, 0), (0, 0), (0, 0), (1, 1)))
    summed = jnp.zeros((inputs.shape[0], extent, inputs.shape[2], across), jnp.float32)
    for row_tap in range(3):
        for col_tap in range(3):
            summed = summed + kernel[:, row_tap, col_tap][:, None, None, None] * padded[
                :, row_tap : row_tap + extent, :, col_tap : col_tap + across
            ].astype(jnp.float32)
    return summed


def conv_depth(inputs, kernel):
    depth_len = inputs.shape[2]
    padded = jnp.pad(inputs, ((0, 0), (0, 0), (1, 1), (0, 0)))
    summed = jnp.zeros(inputs.shape, jnp.float32)
    for depth_tap in range(3):
        summed = (
            summed
            + kernel[:, depth_tap][:, None, None, None]
            * padded[:, :, depth_tap : depth_tap + depth_len, :]
        )
    return summed


def mix_channels(weights, inputs):
    channels = inputs.shape[0]
    flat = inputs.reshape(channels, -1)
    return jnp.dot(weights, flat, preferred_element_type=jnp.float32).reshape(inputs.shape)


def forward_block(inputs, kernel_xy, kernel_z, weights):
    planar = conv_plane(inputs, kernel_xy)
    axial = conv_depth(planar, kernel_z).astype(jnp.bfloat16)
    preact = mix_channels(weights, axial)
    return (planar, axial, preact)


def silu_slope(preact):
    sigma = jax.nn.sigmoid(preact)
    return sigma * (1.0 + preact * (1.0 - sigma))


def backward_block(grad_out, planar, axial, preact, around, kernel_z, weights, trim):
    grad_pre = (grad_out.astype(jnp.float32) * silu_slope(preact)).astype(jnp.bfloat16)
    channels = grad_pre.shape[0]
    grad_axial = jnp.dot(
        weights.T, grad_pre.reshape(channels, -1), preferred_element_type=jnp.float32
    ).reshape(grad_pre.shape)
    grad_planar = conv_depth(grad_axial, kernel_z[:, ::-1]).astype(jnp.bfloat16)
    extent = grad_pre.shape[1]
    own_extent = extent - 2 * trim
    own_pre = grad_pre.reshape(channels, -1)
    own_axial = axial.reshape(channels, -1)
    grad_weights = lax.dot_general(
        own_pre, own_axial, (((1,), (1,)), ((), ())), preferred_element_type=jnp.float32
    )
    depth_len = planar.shape[2]
    planar_pad = jnp.pad(planar, ((0, 0), (0, 0), (1, 1), (0, 0)))
    grad_kz = jnp.stack(
        [
            jnp.sum(
                grad_axial * planar_pad[:, :, depth_tap : depth_tap + depth_len, :], axis=(1, 2, 3)
            )
            for depth_tap in range(3)
        ],
        axis=1,
    )
    own_grad_planar = grad_planar.astype(jnp.float32)
    across = around.shape[3]
    around_pad = jnp.pad(around, ((0, 0), (0, 0), (0, 0), (1, 1)))
    rows_list = []
    for row_tap in range(3):
        cols_list = []
        for col_tap in range(3):
            cols_list.append(
                jnp.sum(
                    own_grad_planar
                    * around_pad[
                        :, row_tap : row_tap + own_extent, :, col_tap : col_tap + across
                    ].astype(jnp.float32),
                    axis=(1, 2, 3),
                )
            )
        rows_list.append(jnp.stack(cols_list, axis=1))
    grad_kxy = jnp.stack(rows_list, axis=1)
    return (grad_planar, (grad_weights, grad_kxy, grad_kz))


def edge_grads(grad_planar):
    return padded_2(grad_planar, (("sp", 1),), 1)


def settle_all(lower, upper):
    summed = lax.psum((lower[0], lower[1], lower[2], upper[0], upper[1], upper[2]), ("sp", "dp"))
    return ((summed[0], summed[1], summed[2]), (summed[3], summed[4], summed[5]))


def on_device(volume, cotangent, kernels_xy, kernels_z, mixing):
    inputs = volume[0]
    grad_top = cotangent[0]
    kernel_xy = kernels_xy.astype(jnp.float32)
    kernel_z = kernels_z.astype(jnp.float32)
    slab_len = inputs.shape[1]
    ranks = lax.axis_size("sp")
    place = lax.axis_index("sp")
    wide = padded_2(inputs, (("sp", 1),), 2)
    planar1, axial1, preact1 = forward_block(wide, kernel_xy[0], kernel_z[0], mixing[0])
    hidden = jax.nn.silu(preact1).astype(jnp.bfloat16)
    spots = place * slab_len - 1 + jnp.arange(slab_len + 2, dtype=jnp.int32)
    hidden = jnp.where(
        ((spots >= 0) & (spots < slab_len * ranks))[None, :, None, None],
        hidden,
        jnp.zeros_like(hidden),
    )
    planar2, axial2, preact2 = forward_block(hidden, kernel_xy[1], kernel_z[1], mixing[1])
    grad_planar2, upper = backward_block(
        grad_top, planar2, axial2, preact2, hidden, kernel_z[1], mixing[1], 0
    )
    grad_hidden = conv_plane(edge_grads(grad_planar2), kernel_xy[1][:, ::-1, ::-1]).astype(
        jnp.bfloat16
    )
    grad_planar1, lower = backward_block(
        grad_hidden,
        planar1[:, 1:-1],
        axial1[:, 1:-1],
        preact1[:, 1:-1],
        wide[:, 1:-1],
        kernel_z[0],
        mixing[0],
        0,
    )
    grad_inputs = conv_plane(edge_grads(grad_planar1), kernel_xy[0][:, ::-1, ::-1]).astype(
        jnp.bfloat16
    )
    lower, upper = settle_all(lower, upper)
    factor = 1.0 / math.sqrt(
        lax.axis_size("dp") * slab_len * ranks * inputs.shape[2] * inputs.shape[3]
    )
    mixing_grad = jnp.stack([lower[0], upper[0]]) * factor
    xy_grad = jnp.stack([lower[1], upper[1]]) * factor
    z_grad = jnp.stack([lower[2], upper[2]]) * factor
    return (grad_inputs[None], mixing_grad, xy_grad, z_grad)


def solution(mesh):
    return jax.shard_map(
        on_device,
        mesh=mesh,
        in_specs=(P("dp", None, "sp", None, None), P("dp", None, "sp", None, None), P(), P(), P()),
        out_specs=(P("dp", None, "sp", None, None), P(), P(), P()),
        check_vma=False,
    )
```

profile of v0, /device:TPU:1, one launch (start us, length us, event | category | flops | bytes accessed | tf_op | source)
XLA Modules:
  0.0 328.5 jit_solution(12075035630448840751)
XLA Ops:
  7.2 0.0 copy-start.7
  7.2 0.0 copy-start.8
  7.2 0.0 copy-start.4
  7.2 0.0 all-reduce.13.cloned.1.call-start
  7.2 1.5 copy.76
  8.7 0.1 fusion.106
  8.8 4.9 %collective-permute-start = (bf16[96,2,8,128]{3,0,2,1:T(8,128)(2,1)S(1)}, bf16[96,2,8,128]{3,0,2,1:T(8,128)(2,1)S(1)}, u32[]{:S(2)}, u32[]{:S(2)}) collective-permute-start(bf16[96,2,8,128]{3,0,2,1:T(8,128)(2,1)S(1)} %get-tuple-element.61), channel_id=1, source_target_pairs={{0,4},{4,8},{8,12},{12,16},{16,20},{20,24},{24,28},{28,32},{32,36}... | collective-permute-start | bytes 1179656 | tf_op jit(solution)/shard_map/ppermute | solution.py:15
  13.8 1.9 collective-permute-start.1
  15.8 0.0 copy-done.4
  15.8 1.5 reshape.101
  17.3 1.2 collective-permute-done
  18.5 4.4 %collective-permute-done.1 = bf16[96,2,8,128]{3,0,2,1:T(8,128)(2,1)S(1)} collective-permute-done((bf16[96,2,8,128]{3,0,2,1:T(8,128)(2,1)S(1)}, bf16[96,2,8,128]{3,0,2,1:T(8,128)(2,1)S(1)}, u32[]{:S(2)}, u32[]{:S(2)}) %collective-permute-start.1) | collective-permute-done | bytes 393248 | tf_op jit(solution)/shard_map/ppermute | solution.py:16
  22.9 0.2 pad_maximum_fusion
  23.0 3.1 multiply_add_fusion
  26.1 1.4 copy-done
  27.5 0.5 fusion.15
  28.1 0.0 copy-start.6
  28.1 0.5 copy.22
  28.5 0.3 copy-done.6
  28.9 0.5 convolution_bitcast_fusion
  29.3 0.4 copy.41
  29.7 0.6 fusion.79
  30.4 3.0 fusion.24
  33.4 0.6 add_convert_fusion
  34.0 0.4 fusion.84
  34.4 1.0 copy-done.5
  35.4 0.8 convolution_bitcast_fusion.2
  36.2 0.3 copy.43
  36.5 6.6 %multiply_reduce_fusion.2 = (f32[96]{0:T(128)S(1)}, f32[96]{0:T(128)S(1)}, f32[96]{0:T(128)S(1)}, f32[96]{0:T(128)S(1)}, f32[96]{0:T(128)S(1)}, /*index=5*/f32[9...) fusion(f32[96,4,8,128]{3,2,1,0:T(8,128)S(1)} %bitcast.196, ...), kind=kLoop, calls=%fused_computation.147 | loop fusion | flops 15727488 | bytes 7477248 | tf_op jit(solution)/shard_map/reduce_sum | solution.py:83
  43.1 1.9 collective-permute-start.2
  45.1 2.6 collective-permute-start.3
  47.7 0.3 copy.46
  47.9 0.6 fusion.69
  48.6 0.6 maximum_bitcast_fusion.9
  49.2 0.6 maximum_bitcast_fusion.1
  49.8 1.2 convolution_bitcast_fusion.3
  51.0 0.0 collective-permute-done.2
  51.0 1.4 collective-permute-done.3
  52.3 1.5 fusion.9
  53.9 3.5 %multiply_convert_fusion.1 = bf16[96,4,8,128]{3,2,1,0:T(8,128)(2,1)S(1)} fusion(f32[96,6,8,128]{3,2,1,0:T(8,128)S(1)} %bitcast.193, bf16[96,6,8,130]{3,2,1,0:T(8,128)(2,1)S(1)} %fusion.9, f32[96]{0:T(128)S(1)} %get-tuple-element.71, bf16[96,1,8,128]{3,2,1,0:T(8,128)(2,1)S(1)} %collective-permute-done.3, bf16[96,4,8,128]{3,2,1,0:T(8,128)(2,1)S(1)} %get-tuple-element.56, ...), kind=kLoop, calls=%fused_computation.149 | loop fusion | flops 15335424 | bytes 8260992 | tf_op jit(solution)/shard_map/convert_element_type | solution.py:66
  57.4 1.0 convolution_bitcast_fusion.4
  58.5 0.4 convolution_bitcast_fusion.1
  58.9 0.0 slice-start
  58.9 0.3 copy.45
  59.2 0.9 copy-done.1
  60.1 0.6 slice-done
  60.7 1.4 fusion.31
  62.1 0.6 maximum_bitcast_fusion.8
  62.7 2.8 fusion.60
  65.5 0.6 maximum_bitcast_fusion
  66.1 0.0 all-reduce.13.cloned.1.call-update
  66.2 2.1 collective-permute-start.4
  68.3 2.3 collective-permute-start.5
  70.6 242.2 %all-reduce.13.cloned.1.call-done = (f32[1,96,96]{2,1,0:T(8,128)}, f32[1,96,96]{2,1,0:T(8,128)}, f32[1,96,3,3]{1,3,2,0:T(4,128)}, f32[1,96,3,3]{1,3,2,0:T(4,128)...) async-done(((f32[1,96,96]{2,1,0:T(8,128)}, f32[1,96,96]{2,1,0:T(8,128)}, f32[1,96,3,3]{1,3,2,0:T(4,128)}, f32[1,96,3,3]{1,3,2,0:T(4,128)}, f32[1,96,3]{1,2,0:T(4,128)}, ...) | async-done | bytes 82960 | tf_op jit(solution)/shard_map/psum | solution.py:116
  312.8 0.7 maximum_multiply_fusion.2
  313.5 0.6 copy.33
  314.1 0.7 maximum_multiply_fusion.1
  314.8 0.6 copy.32
  315.4 1.5 maximum_multiply_fusion
  316.9 0.0 collective-permute-done.4
  316.9 0.0 collective-permute-done.5
  316.9 1.6 fusion.11
  318.4 2.0 fusion.92
  320.4 1.2 copy.31
  (28 shorter events, 0.2 us)
Async XLA Ops:
  7.2 8.5 %copy-start.7 = (bf16[2,96,3,3]{1,0,3,2:T(2,128)(2,1)S(1)}, bf16[2,96,3,3]{1,0,3,2:T(2,128)(2,1)}, u32[]{:S(2)}) copy-start(bf16[2,96,3,3]{1,0,3,2:T(2,128)(2,1)} %param.7) | copy-start | bytes 10372
  7.2 8.6 %copy-start.8 = (bf16[2,96,3]{1,0,2:T(2,128)(2,1)S(1)}, bf16[2,96,3]{1,0,2:T(2,128)(2,1)}, u32[]{:S(2)}) copy-start(bf16[2,96,3]{1,0,2:T(2,128)(2,1)} %param.8) | copy-start | bytes 3460
  7.2 8.6 %copy-start.4 = (bf16[1,96,4,8,128]{4,3,2,1,0:T(8,128)(2,1)S(1)}, bf16[1,96,4,8,128]{4,3,2,1,0:T(8,128)(2,1)}, u32[]{:S(2)}) copy-start(bf16[1,96,4,8,128]{4,3,2,1,0:T(8,128)(2,1)} %param.6) | copy-start | bytes 2359300
  7.2 305.6 %all-reduce.13.cloned.1.call-start = ((), (), s32[]{:S(2)}) async-start(), calls=%async_computation | async-start | bytes 229376 | tf_op jit(solution)/shard_map/psum | solution.py:116
  8.8 9.6 %collective-permute-start = (bf16[96,2,8,128]{3,0,2,1:T(8,128)(2,1)S(1)}, bf16[96,2,8,128]{3,0,2,1:T(8,128)(2,1)S(1)}, u32[]{:S(2)}, u32[]{:S(2)}) collective-permute-start(bf16[96,2,8,128]{3,0,2,1:T(8,128)(2,1)S(1)} %get-tuple-element.61), channel_id=1, source_target_pairs={{0,4},{4,8},{8,12},{12,16},{16,20},{20,24},{24,28},{28,32},{32,36}... | collective-permute-start | bytes 1179656 | tf_op jit(solution)/shard_map/ppermute | solution.py:15
  13.8 9.1 %collective-permute-start.1 = (bf16[96,2,8,128]{3,0,2,1:T(8,128)(2,1)S(1)}, bf16[96,2,8,128]{3,0,2,1:T(8,128)(2,1)S(1)}, u32[]{:S(2)}, u32[]{:S(2)}) collective-permute-start(bf16[96,2,8,128]{3,0,2,1:T(8,128)(2,1)S(1)} %get-tuple-element.62), channel_id=1, source_target_pairs={{4,0},{8,4},{12,8},{16,12},{20,16},{24,20},{28,24},{32,28},{36,32}... | collective-permute-start | bytes 1179656 | tf_op jit(solution)/shard_map/ppermute | solution.py:16
  23.0 3.1 copy-start.2
  26.1 1.4 copy-start
  28.1 0.8 copy-start.6
  34.0 1.4 copy-start.5
  43.1 7.8 %collective-permute-start.2 = (bf16[96,1,8,128]{3,2,1,0:T(8,128)(2,1)S(1)}, bf16[96,1,8,128]{3,2,1,0:T(8,128)(2,1)S(1)}, u32[]{:S(2)}, u32[]{:S(2)}) collective-permute-start(bf16[96,1,8,128]{3,2,1,0:T(8,128)(2,1)S(1)} %get-tuple-element.59), channel_id=1, source_target_pairs={{0,4},{4,8},{8,12},{12,16},{16,20},{20,24},{24,28},{28,32},{32,36}... | collective-permute-start | bytes 589832 | tf_op jit(solution)/shard_map/ppermute | solution.py:15
  45.1 7.3 %collective-permute-start.3 = (bf16[96,1,8,128]{3,2,1,0:T(8,128)(2,1)S(1)}, bf16[96,1,8,128]{3,2,1,0:T(8,128)(2,1)S(1)}, u32[]{:S(2)}, u32[]{:S(2)}) collective-permute-start(bf16[96,1,8,128]{3,2,1,0:T(8,128)(2,1)S(1)} %get-tuple-element.60), channel_id=1, source_target_pairs={{4,0},{8,4},{12,8},{16,12},{20,16},{24,20},{28,24},{32,28},{36,32}... | collective-permute-start | bytes 589832 | tf_op jit(solution)/shard_map/ppermute | solution.py:16
  58.5 1.7 copy-start.1
  58.9 1.8 slice-start
  60.7 2.0 slice-start.1
  60.7 2.0 copy-start.3
  66.2 250.6 %collective-permute-start.4 = (bf16[96,1,8,128]{3,0,2,1:T(8,128)(2,1)S(1)}, bf16[96,1,8,128]{3,0,2,1:T(8,128)(2,1)S(1)}, u32[]{:S(2)}, u32[]{:S(2)}) collective-permute-start(bf16[96,1,8,128]{3,0,2,1:T(8,128)(2,1)S(1)} %get-tuple-element.57), channel_id=1, source_target_pairs={{0,4},{4,8},{8,12},{12,16},{16,20},{20,24},{24,28},{28,32},{32,36}... | collective-permute-start | bytes 589832 | tf_op jit(solution)/shard_map/ppermute | solution.py:15
  68.3 248.6 %collective-permute-start.5 = (bf16[96,1,8,128]{3,0,2,1:T(8,128)(2,1)S(1)}, bf16[96,1,8,128]{3,0,2,1:T(8,128)(2,1)S(1)}, u32[]{:S(2)}, u32[]{:S(2)}) collective-permute-start(bf16[96,1,8,128]{3,0,2,1:T(8,128)(2,1)S(1)} %get-tuple-element.58), channel_id=1, source_target_pairs={{4,0},{8,4},{12,8},{16,12},{20,16},{24,20},{28,24},{32,28},{36,32}... | collective-permute-start | bytes 589832 | tf_op jit(solution)/shard_map/ppermute | solution.py:16
Sparse Core Ops, SparseCore 0:
  66.3 246.4 all-reduce.12
where the time goes:
time: 329 us; the launch traced here: 328 us
  waiting for transfers between devices  249 us (76%)
  other arithmetic  33.4 us (10%)
  starting transfers between devices  15.7 us (5%)
  between operations  14.4 us (4%)
  local copies, waits for them, and re-layouts  11.5 us (3%)
  matrix products  4.28 us (1%)
    psum x1, waiting for transfers between devices, settle_all(): lax.psum((lower[0], lower[1], lower[2], upper[0], upper[1], upper[2]), ('...  242 us
    ppermute x3, starting transfers between devices, padded_2(): before = lax.ppermute(last, axis, up)  8.92 us
    unnamed x28, local copies, waits for them, and re-layouts  8.82 us
    reduce_sum x2, other arithmetic, backward_block(): jnp.sum(grad_axial * planar_pad[:, :, depth_tap:depth_tap + depth_len, :]...  7.96 us
    ppermute x3, starting transfers between devices, padded_2(): after = lax.ppermute(first, axis, down)  6.79 us
  transfers between devices with their start and end apart: 7, of which 4 were waited for; matrix products, arithmetic and copies ran while one was open for 3% of the time, Pallas kernels for 0%

commit v1 on v0

--- a/solution.py
+++ b/solution.py
@@ -3,6 +3,7 @@
 import jax.numpy as jnp
 from jax import lax
 from jax.sharding import PartitionSpec as P
+from jax.lax import psum
 
 
 def padded_2(x, sides, width):
@@ -113,7 +114,12 @@
 
 
 def settle_all(lower, upper):
-    summed = lax.psum((lower[0], lower[1], lower[2], upper[0], upper[1], upper[2]), ("sp", "dp"))
+
+    def knots_post(message):
+        main = psum(psum(message, axis_name="dp"), axis_name="sp")
+        return main
+
+    summed = knots_post((lower[0], lower[1], lower[2], upper[0], upper[1], upper[2]))
     return ((summed[0], summed[1], summed[2]), (summed[3], summed[4], summed[5]))
 
 

time: 329 us -> 310 us (0.942)
  waiting for transfers between devices: 249 us -> 227 us
  starting transfers between devices: 15.7 us -> 19.3 us
    psum x1 -> x2, waiting for transfers between devices: 242 us -> 220 us  [knots_post(): main = psum(psum(message, axis_name='dp'), axis_name='sp')]
    ppermute x3, starting transfers between devices: 8.92 us -> 12.8 us  [padded_2(): before = lax.ppermute(last, axis, up)]
  transfers between devices with their start and end apart: 7 -> 8, of which waited for: 4 -> 5; matrix products, arithmetic and copies ran while one was open for 3% -> 3% of each run, Pallas kernels for 0% -> 0%
where the time goes in v1:
time: 310 us
  waiting for transfers between devices  227 us (73%)
  other arithmetic  33.3 us (11%)
  starting transfers between devices  19.3 us (6%)
  between operations  14.5 us (5%)
  local copies, waits for them, and re-layouts  11.5 us (4%)
  matrix products  4.28 us (1%)
    psum x2, waiting for transfers between devices, knots_post(): main = psum(psum(message, axis_name='dp'), axis_name='sp')  220 us
    ppermute x3, starting transfers between devices, padded_2(): before = lax.ppermute(last, axis, up)  12.8 us
    unnamed x28, local copies, waits for them, and re-layouts  8.82 us
    reduce_sum x2, other arithmetic, backward_block(): jnp.sum(grad_axial * planar_pad[:, :, depth_tap:depth_tap + depth_len, :]...  7.96 us
    ppermute x3, starting transfers between devices, padded_2(): after = lax.ppermute(first, axis, down)  6.44 us
  transfers between devices with their start and end apart: 8, of which 5 were waited for; matrix products, arithmetic and copies ran while one was open for 3% of the time, Pallas kernels for 0%

profile of v1, /device:TPU:1, one launch (start us, length us, event | category | flops | bytes accessed | tf_op | source)
XLA Modules:
  0.0 309.6 jit_solution(15040629994780435620)
XLA Ops:
  7.2 0.0 copy-start.7
  7.2 0.0 all-reduce.17.cloned.1.call-start
  7.2 1.5 copy.76
  8.7 0.1 fusion.106
  8.8 4.9 %collective-permute-start = (bf16[96,2,8,128]{3,0,2,1:T(8,128)(2,1)S(1)}, bf16[96,2,8,128]{3,0,2,1:T(8,128)(2,1)S(1)}, u32[]{:S(2)}, u32[]{:S(2)}) collective-permute-start(bf16[96,2,8,128]{3,0,2,1:T(8,128)(2,1)S(1)} %get-tuple-element.67), channel_id=1, source_target_pairs={{0,4},{4,8},{8,12},{12,16},{16,20},{20,24},{24,28},{28,32},{32,36}... | collective-permute-start | bytes 1179656 | tf_op jit(solution)/shard_map/ppermute | solution.py:16
  13.8 1.9 collective-permute-start.1
  15.8 1.5 reshape.101
  17.3 1.2 collective-permute-done
  18.5 4.4 %collective-permute-done.1 = bf16[96,2,8,128]{3,0,2,1:T(8,128)(2,1)S(1)} collective-permute-done((bf16[96,2,8,128]{3,0,2,1:T(8,128)(2,1)S(1)}, bf16[96,2,8,128]{3,0,2,1:T(8,128)(2,1)S(1)}, u32[]{:S(2)}, u32[]{:S(2)}) %collective-permute-start.1) | collective-permute-done | bytes 393248 | tf_op jit(solution)/shard_map/ppermute | solution.py:17
  22.9 0.2 pad_maximum_fusion
  23.0 3.1 multiply_add_fusion
  26.1 1.4 copy-done
  27.5 0.5 fusion.15
  28.1 0.0 copy-start.6
  28.1 0.5 copy.22
  28.5 0.3 copy-done.6
  28.9 0.5 convolution_bitcast_fusion
  29.3 0.4 copy.41
  29.7 0.6 fusion.79
  30.4 3.0 fusion.24
  33.4 0.6 add_convert_fusion
  34.0 0.4 fusion.84
  34.4 1.0 copy-done.5
  35.4 0.8 convolution_bitcast_fusion.2
  36.2 0.3 copy.43
  36.5 6.6 %multiply_reduce_fusion.2 = (f32[96]{0:T(128)S(1)}, f32[96]{0:T(128)S(1)}, f32[96]{0:T(128)S(1)}, f32[96]{0:T(128)S(1)}, f32[96]{0:T(128)S(1)}, /*index=5*/f32[9...) fusion(f32[96,4,8,128]{3,2,1,0:T(8,128)S(1)} %bitcast.190, ...), kind=kLoop, calls=%fused_computation.147 | loop fusion | flops 15727488 | bytes 7477248 | tf_op jit(solution)/shard_map/reduce_sum | solution.py:84
  43.1 1.9 collective-permute-start.2
  45.1 2.6 collective-permute-start.3
  47.7 0.3 copy.46
  47.9 0.6 fusion.69
  48.6 0.6 pad_maximum_fusion.10
  49.2 0.6 pad_maximum_fusion.8
  49.8 1.2 convolution_bitcast_fusion.3
  51.0 0.0 collective-permute-done.2
  51.0 1.4 collective-permute-done.3
  52.3 1.5 fusion.9
  53.9 3.5 %multiply_convert_fusion.1 = bf16[96,4,8,128]{3,2,1,0:T(8,128)(2,1)S(1)} fusion(f32[96,6,8,128]{3,2,1,0:T(8,128)S(1)} %bitcast.187, bf16[96,6,8,130]{3,2,1,0:T(8,128)(2,1)S(1)} %fusion.9, f32[96]{0:T(128)S(1)} %get-tuple-element.77, bf16[96,1,8,128]{3,2,1,0:T(8,128)(2,1)S(1)} %collective-permute-done.3, bf16[96,4,8,128]{3,2,1,0:T(8,128)(2,1)S(1)} %get-tuple-element.62, ...), kind=kLoop, calls=%fused_computation.149 | loop fusion | flops 15335424 | bytes 8260992 | tf_op jit(solution)/shard_map/convert_element_type | solution.py:67
  57.4 1.0 convolution_bitcast_fusion.4
  58.5 0.4 convolution_bitcast_fusion.1
  58.9 0.0 slice-start
  58.9 0.3 copy.45
  59.2 0.9 copy-done.1
  60.1 0.6 slice-done
  60.7 1.4 fusion.31
  62.1 0.6 pad_maximum_fusion.9
  62.7 2.8 fusion.60
  65.5 0.6 pad_maximum_fusion.7
  66.1 0.0 all-reduce.17.cloned.1.call-update
  66.1 0.0 all-reduce.15.cloned.1.call-start
  66.2 47.1 %all-reduce.17.cloned.1.call-done = (f32[96,96]{1,0:T(8,128)}, f32[96,96]{1,0:T(8,128)}, f32[96,3,3]{0,2,1:T(4,128)}, f32[96,3,3]{0,2,1:T(4,128)}, f32[96,3]{0,1:T(4,128)}, /*index=5*/f32[96,3]{0,1:T(4,128)}) async-done(((f32[96,96]{1,0:T(8,128)}, f32[96,96]{1,0:T(8,128)}, f32[96,3,3]{0,2,1:T(4,128)}, f32[96,3,3]{0,2,1:T(4,128)}, f32[96,3]{0,1:T(4,128)}, /*index=5*/f32[96,3]{0,1:T(4,128)}), ...) | async-done | bytes 82960 | tf_op jit(solution)/shard_map/psum | solution.py:119
  113.3 0.0 all-reduce.15.cloned.1.call-update
  113.4 5.9 %collective-permute-start.4 = (bf16[96,1,8,128]{3,0,2,1:T(8,128)(2,1)S(1)}, bf16[96,1,8,128]{3,0,2,1:T(8,128)(2,1)S(1)}, u32[]{:S(2)}, u32[]{:S(2)}) collective-permute-start(bf16[96,1,8,128]{3,0,2,1:T(8,128)(2,1)S(1)} %get-tuple-element.63), channel_id=1, source_target_pairs={{0,4},{4,8},{8,12},{12,16},{16,20},{20,24},{24,28},{28,32},{32,36}... | collective-permute-start | bytes 589832 | tf_op jit(solution)/shard_map/ppermute | solution.py:16
  119.3 1.9 collective-permute-start.5
  121.2 172.8 %all-reduce.15.cloned.1.call-done = (f32[1,96,96]{2,1,0:T(8,128)}, f32[1,96,96]{2,1,0:T(8,128)}, f32[1,96,3,3]{1,3,2,0:T(4,128)}, f32[1,96,3,3]{1,3,2,0:T(4,128)...) async-done(((f32[1,96,96]{2,1,0:T(8,128)}, f32[1,96,96]{2,1,0:T(8,128)}, f32[1,96,3,3]{1,3,2,0:T(4,128)}, f32[1,96,3,3]{1,3,2,0:T(4,128)}, f32[1,96,3]{1,2,0:T(4,128)}, ...) | async-done | bytes 82960 | tf_op jit(solution)/shard_map/psum | solution.py:119
  294.0 0.7 maximum_multiply_fusion.2
  294.7 0.6 copy.33
  295.2 0.7 maximum_multiply_fusion.1
  295.9 0.6 copy.32
  296.6 1.5 maximum_multiply_fusion
  298.0 0.0 collective-permute-done.4
  298.0 0.0 collective-permute-done.5
  298.0 1.6 fusion.11
  299.6 2.0 fusion.92
  301.6 1.2 copy.31
  (31 shorter events, 0.2 us)
Async XLA Ops:
  7.2 8.5 %copy-start.7 = (bf16[2,96,3,3]{1,0,3,2:T(2,128)(2,1)S(1)}, bf16[2,96,3,3]{1,0,3,2:T(2,128)(2,1)}, u32[]{:S(2)}) copy-start(bf16[2,96,3,3]{1,0,3,2:T(2,128)(2,1)} %param.7) | copy-start | bytes 10372
  7.2 8.6 %copy-start.8 = (bf16[2,96,3]{1,0,2:T(2,128)(2,1)S(1)}, bf16[2,96,3]{1,0,2:T(2,128)(2,1)}, u32[]{:S(2)}) copy-start(bf16[2,96,3]{1,0,2:T(2,128)(2,1)} %param.8) | copy-start | bytes 3460
  7.2 8.6 %copy-start.4 = (bf16[1,96,4,8,128]{4,3,2,1,0:T(8,128)(2,1)S(1)}, bf16[1,96,4,8,128]{4,3,2,1,0:T(8,128)(2,1)}, u32[]{:S(2)}) copy-start(bf16[1,96,4,8,128]{4,3,2,1,0:T(8,128)(2,1)} %param.6) | copy-start | bytes 2359300
  7.2 106.1 %all-reduce.17.cloned.1.call-start = ((), (), s32[]{:S(2)}) async-start(), calls=%async_computation.1 | async-start | bytes 229376 | tf_op jit(solution)/shard_map/psum | solution.py:119
  8.8 9.6 %collective-permute-start = (bf16[96,2,8,128]{3,0,2,1:T(8,128)(2,1)S(1)}, bf16[96,2,8,128]{3,0,2,1:T(8,128)(2,1)S(1)}, u32[]{:S(2)}, u32[]{:S(2)}) collective-permute-start(bf16[96,2,8,128]{3,0,2,1:T(8,128)(2,1)S(1)} %get-tuple-element.67), channel_id=1, source_target_pairs={{0,4},{4,8},{8,12},{12,16},{16,20},{20,24},{24,28},{28,32},{32,36}... | collective-permute-start | bytes 1179656 | tf_op jit(solution)/shard_map/ppermute | solution.py:16
  13.8 9.1 %collective-permute-start.1 = (bf16[96,2,8,128]{3,0,2,1:T(8,128)(2,1)S(1)}, bf16[96,2,8,128]{3,0,2,1:T(8,128)(2,1)S(1)}, u32[]{:S(2)}, u32[]{:S(2)}) collective-permute-start(bf16[96,2,8,128]{3,0,2,1:T(8,128)(2,1)S(1)} %get-tuple-element.68), channel_id=1, source_target_pairs={{4,0},{8,4},{12,8},{16,12},{20,16},{24,20},{28,24},{32,28},{36,32}... | collective-permute-start | bytes 1179656 | tf_op jit(solution)/shard_map/ppermute | solution.py:17
  23.0 3.1 copy-start.2
  26.1 1.4 copy-start
  28.1 0.8 copy-start.6
  34.0 1.4 copy-start.5
  43.1 7.8 %collective-permute-start.2 = (bf16[96,1,8,128]{3,2,1,0:T(8,128)(2,1)S(1)}, bf16[96,1,8,128]{3,2,1,0:T(8,128)(2,1)S(1)}, u32[]{:S(2)}, u32[]{:S(2)}) collective-permute-start(bf16[96,1,8,128]{3,2,1,0:T(8,128)(2,1)S(1)} %get-tuple-element.65), channel_id=1, source_target_pairs={{0,4},{4,8},{8,12},{12,16},{16,20},{20,24},{24,28},{28,32},{32,36}... | collective-permute-start | bytes 589832 | tf_op jit(solution)/shard_map/ppermute | solution.py:16
  45.1 7.3 %collective-permute-start.3 = (bf16[96,1,8,128]{3,2,1,0:T(8,128)(2,1)S(1)}, bf16[96,1,8,128]{3,2,1,0:T(8,128)(2,1)S(1)}, u32[]{:S(2)}, u32[]{:S(2)}) collective-permute-start(bf16[96,1,8,128]{3,2,1,0:T(8,128)(2,1)S(1)} %get-tuple-element.66), channel_id=1, source_target_pairs={{4,0},{8,4},{12,8},{16,12},{20,16},{24,20},{28,24},{32,28},{36,32}... | collective-permute-start | bytes 589832 | tf_op jit(solution)/shard_map/ppermute | solution.py:17
  58.5 1.7 copy-start.1
  58.9 1.8 slice-start
  60.7 2.0 slice-start.1
  60.7 2.0 copy-start.3
  66.1 227.8 %all-reduce.15.cloned.1.call-start = ((), (), s32[]{:S(2)}) async-start(), calls=%async_computation | async-start | bytes 229376 | tf_op jit(solution)/shard_map/psum | solution.py:119
  113.4 184.7 %collective-permute-start.4 = (bf16[96,1,8,128]{3,0,2,1:T(8,128)(2,1)S(1)}, bf16[96,1,8,128]{3,0,2,1:T(8,128)(2,1)S(1)}, u32[]{:S(2)}, u32[]{:S(2)}) collective-permute-start(bf16[96,1,8,128]{3,0,2,1:T(8,128)(2,1)S(1)} %get-tuple-element.63), channel_id=1, source_target_pairs={{0,4},{4,8},{8,12},{12,16},{16,20},{20,24},{24,28},{28,32},{32,36}... | collective-permute-start | bytes 589832 | tf_op jit(solution)/shard_map/ppermute | solution.py:16
  119.3 178.8 %collective-permute-start.5 = (bf16[96,1,8,128]{3,0,2,1:T(8,128)(2,1)S(1)}, bf16[96,1,8,128]{3,0,2,1:T(8,128)(2,1)S(1)}, u32[]{:S(2)}, u32[]{:S(2)}) collective-permute-start(bf16[96,1,8,128]{3,0,2,1:T(8,128)(2,1)S(1)} %get-tuple-element.64), channel_id=1, source_target_pairs={{4,0},{8,4},{12,8},{16,12},{20,16},{24,20},{28,24},{32,28},{36,32}... | collective-permute-start | bytes 589832 | tf_op jit(solution)/shard_map/ppermute | solution.py:17
Sparse Core Ops, SparseCore 0:
  66.3 47.0 all-reduce.16
  118.1 175.7 all-reduce.14
